TPU v7x, 256 devices: a whole 4x4x8 slice. The times are simulated.
256 devices in a mesh: dp: 2 (over z_lo), node: 16 (over x, z_hi), local: 8 (over y, core).
Axes of the slice: x: 4, y: 4, z: 8 (z_hi: 4, z_lo: 2; z = z_hi * 2 + z_lo), core: 2. Of those that a mesh axis runs over, the one named last changes fastest.
Arguments:
- tokens_in: bfloat16 [2, 16, 64, 16, 3584], P('dp', 'node'), may hold values from -6 to 6
- grad_rows: bfloat16 [2, 16, 64, 16, 3584], P('dp', 'node'), may hold values from -6 to 6
- combine_weights: float32 [2, 16, 64, 16], P('dp', 'node'), may hold values from 0.05 to 1
- live_counts: int32 [2, 16, 16], P('dp', 'node'), may hold values from 0 to 64, as said below
- w_gate: bfloat16 [16, 3584, 2048], P('node', None, 'local'), may hold values from -0.09375 to 0.09375
- w_up: bfloat16 [16, 3584, 2048], P('node', None, 'local'), may hold values from -0.09375 to 0.09375
- w_down: bfloat16 [16, 3584, 2048], P('node', None, 'local'), may hold values from -0.125 to 0.125
Outputs:
- d_tokens: bfloat16 [2, 16, 64, 16, 3584], P('dp', 'node', 'local')
- grad_gate: bfloat16 [16, 3584, 2048], P('node', 'dp', 'local')
- grad_up: bfloat16 [16, 3584, 2048], P('node', 'dp', 'local')
- grad_down: bfloat16 [16, 3584, 2048], P('node', 'dp', 'local')
Inputs may be any that keep to these rules, and one draw needn't show every extreme that they name: `live_counts`: each replica has some source and expert pair with all 64 slots live; loads differ strongly between experts.
All inputs are finite; a program needn't handle non-finite values.
Results may differ from a plain program's by a relative error of at most 0.019.
Values may be sent and summed in bfloat16 or wider, within the bound.
A program may use at most 128 MiB of HBM per device.

v0:
```python
import jax
import jax.numpy as jnp
from jax import lax
from jax.sharding import PartitionSpec as P


def on_device(tokens_in, grad_rows, combine_weights, live_counts, w_gate, w_up, w_down):
    slot_count = tokens_in.shape[2]
    node_count = tokens_in.shape[3]
    feature_width = tokens_in.shape[4]
    gate_weight = w_gate[0]
    up_weight = w_up[0]
    down_weight = w_down[0]
    hid_local = gate_weight.shape[1]
    live_mask = (
        lax.broadcasted_iota(jnp.int32, (slot_count, node_count), 0) < live_counts[0, 0][None, :]
    ).astype(jnp.float32)
    scaled_rows = (
        grad_rows[0, 0].astype(jnp.float32) * (combine_weights[0, 0] * live_mask)[:, :, None]
    ).astype(jnp.bfloat16)
    scaled_rows = scaled_rows.reshape(slot_count * node_count, feature_width)
    flat_tokens = tokens_in[0, 0].reshape(slot_count * node_count, feature_width)
    gate_pre = jnp.dot(flat_tokens, gate_weight, preferred_element_type=jnp.float32)
    up_pre = jnp.dot(flat_tokens, up_weight, preferred_element_type=jnp.float32)
    sigmoid_gate = jax.nn.sigmoid(gate_pre)
    activated = gate_pre * sigmoid_gate
    hidden = (activated * up_pre).astype(jnp.bfloat16)
    hidden_grad = jnp.dot(scaled_rows, down_weight, preferred_element_type=jnp.float32)
    gate_grad = (
        hidden_grad * up_pre * sigmoid_gate * (1.0 + gate_pre * (1.0 - sigmoid_gate))
    ).astype(jnp.bfloat16)
    up_grad = (hidden_grad * activated).astype(jnp.bfloat16)
    joined_grad = jnp.concatenate((gate_grad, up_grad), axis=1)
    keep_rows = slot_count // lax.axis_size("local")
    total = lax.dot_general(
        gate_grad, gate_weight, (((1,), (1,)), ((), ())), preferred_element_type=jnp.float32
    )
    total = total + lax.dot_general(
        up_grad, up_weight, (((1,), (1,)), ((), ())), preferred_element_type=jnp.float32
    )
    summed = lax.psum_scatter(
        total.reshape(lax.axis_size("local") * keep_rows, node_count, feature_width).astype(
            jnp.bfloat16
        ),
        "local",
        scatter_dimension=0,
        tiled=True,
    )
    returned = lax.all_to_all(summed, "node", split_axis=1, concat_axis=1, tiled=True)
    d_tokens = returned[None, None]
    front = lax.dot_general(
        flat_tokens, joined_grad, (((0,), (0,)), ((), ())), preferred_element_type=jnp.float32
    )
    behind = lax.dot_general(
        scaled_rows, hidden, (((0,), (0,)), ((), ())), preferred_element_type=jnp.float32
    )
    weight_sums = lax.psum_scatter(
        jnp.concatenate((front, behind), axis=1).astype(jnp.bfloat16),
        "dp",
        scatter_dimension=0,
        tiled=True,
    ).astype(jnp.float32)
    grad_gate = weight_sums[:, :hid_local].astype(jnp.bfloat16)[None]
    grad_up = weight_sums[:, hid_local : 2 * hid_local].astype(jnp.bfloat16)[None]
    grad_down = weight_sums[:, 2 * hid_local :].astype(jnp.bfloat16)[None]
    return (d_tokens, grad_gate, grad_up, grad_down)


def solution(mesh):
    return jax.shard_map(
        on_device,
        mesh=mesh,
        in_specs=(
            P("dp", "node", None, None, None),
            P("dp", "node", None, None, None),
            P("dp", "node", None, None),
            P("dp", "node", None),
            P("node", None, "local"),
            P("node", None, "local"),
            P("node", None, "local"),
        ),
        out_specs=(
            P("dp", "node", "local", None, None),
            P("node", "dp", "local"),
            P("node", "dp", "local"),
            P("node", "dp", "local"),
        ),
        check_vma=False,
    )
```

profile of v0, /device:TPU:1, one launch (start us, length us, event | category | flops | bytes accessed | tf_op | source)
XLA Modules:
  0.0 213.1 jit_solution(1930631063470694649)
XLA Ops:
  7.2 0.0 copy-start
  7.2 0.0 reduce-scatter.7.cloned.1.call-start
  7.2 1.4 copy-done
  8.7 0.0 copy-start.2
  8.7 0.0 copy-start.6
  8.7 6.3 %fusion.4 = f32[1024,256]{0,1:T(8,128)} fusion(bf16[1024,3584]{1,0:T(8,128)(2,1)} %bitcast.56, bf16[1,3584,256]{2,1,0:T(8,128)(2,1)S(1)} %copy-done), kind=kOutput, calls=%fused_computation.10 | convolution fusion | flops 1879048192 | bytes 10223616 | tf_op jit(solution)/shard_map/dot_general | solution.py:23
  15.0 0.0 copy-done.2
  15.0 0.0 copy-done.6
  15.0 0.0 copy-start.4
  15.0 0.0 copy-start.5
  15.0 3.1 %fusion.7 = f32[1024,256]{0,1:T(8,128)} fusion(bf16[1024,3584]{1,0:T(8,128)(2,1)S(1)} %bitcast.58, bf16[1,3584,256]{2,1,0:T(8,128)(2,1)S(1)} %copy-done.2), kind=kOutput, calls=%fused_computation.13 | convolution fusion | flops 1879048192 | bytes 10223616 | tf_op jit(solution)/shard_map/dot_general | solution.py:24
  18.1 0.0 copy-done.4
  18.1 0.0 copy-done.5
  18.1 0.1 bitcast_select_fusion
  18.2 0.1 copy.27
  18.2 5.6 %multiply_convert_fusion = bf16[1,1,64,16,3584]{4,3,2,1,0:T(8,128)(2,1)S(1)} fusion(f32[64,16]{1,0:T(8,128)S(1)} %copy.27, bf16[1,1,64,16,3584]{4,3,2,1,0:T(8,128)(2,1)} %param.8), kind=kLoop, calls=%fused_computation.3 | loop fusion | flops 11010048 | bytes 14684160 | tf_op jit(solution)/shard_map/convert_element_type | solution.py:20
  23.8 4.5 %multiply_convert_fusion.2 = (bf16[1024,256]{0,1:T(8,128)(2,1)S(1)}, bf16[1024,256]{0,1:T(8,128)(2,1)S(1)}) fusion(f32[1024,256]{0,1:T(8,128)} %fusion.4, f32[1024,256]{0,1:T(8,128)} %fusion.7, bf16[1024,3584]{1,0:T(8,128)(2,1)S(1)} %bitcast.51, bf16[1,3584,256]{2,1,0:T(8,128)(2,1)} %param.13), kind=kOutput, calls=%fused_computation.21 | convolution fusion | flops 1882456064 | bytes 12320768 | tf_op jit(solution)/shard_map/dot_general | solution.py:28
  28.3 0.0 copy-start.3
  28.4 7.3 %fusion.2 = f32[1024,3584]{1,0:T(8,128)} fusion(bf16[1024,256]{0,1:T(8,128)(2,1)S(1)} %get-tuple-element.24, bf16[1,3584,256]{2,1,0:T(8,128)(2,1)S(1)} %copy-done), kind=kOutput, calls=%fused_computation.8 | convolution fusion | flops 1879048192 | bytes 17039360 | tf_op jit(solution)/shard_map/dot_general | solution.py:35
  35.7 0.0 copy-done.3
  35.7 7.5 %add_convert_fusion = bf16[1024,3584]{1,0:T(8,128)(2,1)S(1)} fusion(f32[1024,3584]{1,0:T(8,128)} %fusion.2, bf16[1024,256]{0,1:T(8,128)(2,1)S(1)} %get-tuple-element.23, bf16[1,3584,256]{2,1,0:T(8,128)(2,1)S(1)} %copy-done.3), kind=kOutput, calls=%fused_computation.2 | convolution fusion | flops 1886388224 | bytes 24379392 | tf_op jit(solution)/shard_map/dot_general | solution.py:38
  43.2 7.1 %copy.36 = bf16[8,8,16,3584]{3,1,2,0:T(8,128)(2,1)} copy(bf16[8,8,16,3584]{3,2,1,0:T(8,128)(2,1)S(1)} %bitcast.50) | data formatting | bytes 14680064
  50.4 0.0 reduce-scatter.7.cloned.1.call-update
  50.4 0.0 reduce-scatter.5.cloned.1.call-start
  50.4 0.1 copy.29
  50.5 0.1 squeeze.19
  50.6 0.1 iota.15
  50.7 0.1 lt.25
  50.8 5.5 %fusion = bf16[1024,3584]{1,0:T(8,128)(2,1)S(1)} fusion(f32[1024]{0:T(1024)S(1)} %compare_select_fusion, bf16[1,1,64,16,3584]{4,3,2,1,0:T(8,128)(2,1)} %param.8), kind=kLoop, calls=%fused_computation.1 | loop fusion | flops 11010048 | bytes 14684160 | tf_op jit(solution)/shard_map/convert_element_type | solution.py:20
  56.3 3.7 %convolution_convert_fusion.1 = bf16[3584,256]{0,1:T(8,128)(2,1)S(1)} fusion(bf16[1024,3584]{1,0:T(8,128)(2,1)S(1)} %fusion, f32[1024,256]{0,1:T(8,128)} %fusion.7, f32[1024,256]{0,1:T(8,128)} %fusion.4), kind=kOutput, calls=%fused_computation.7 | convolution fusion | flops 1881538560 | bytes 11272192 | tf_op jit(solution)/shard_map/dot_general | solution.py:54
  60.0 7.8 %fusion.1 = bf16[3584,512]{0,1:T(8,128)(2,1)S(1)} fusion(bf16[1024,3584]{1,0:T(8,128)(2,1)} %bitcast.57, bf16[1024,256]{0,1:T(8,128)(2,1)S(1)} %get-tuple-element.23, bf16[1024,256]{0,1:T(8,128)(2,1)S(1)} %get-tuple-element.24), kind=kOutput, calls=%fused_computation.6 | convolution fusion | flops 3762028544 | bytes 12058624 | tf_op jit(solution)/shard_map/dot_general | solution.py:51
  67.8 2.7 %pad_maximum_fusion = bf16[3584,768]{0,1:T(8,128)(2,1)} fusion(bf16[3584,256]{0,1:T(8,128)(2,1)S(1)} %convolution_convert_fusion.1, bf16[3584,512]{0,1:T(8,128)(2,1)S(1)} %fusion.1), kind=kLoop, calls=%fused_computation.5 | loop fusion | flops 11010048 | bytes 11010048 | tf_op jit(solution)/shard_map/concatenate | solution.py:58
  70.5 0.0 reduce-scatter.5.cloned.1.call-update
  70.6 33.2 %reduce-scatter.7.cloned.1.call-done = bf16[8,57344]{1,0:T(8,128)(2,1)} async-done(((bf16[64,57344]{1,0:T(8,128)(2,1)}), bf16[8,57344]{1,0:T(8,128)(2,1)}) %reduce-scatter.7.cloned.1.call-update) | async-done | bytes 917520
  103.8 0.0 copy-start.1
  103.8 9.4 %all-to-all-start = ((bf16[8,16,3584]{2,0,1:T(8,128)(2,1)}), bf16[8,16,3584]{2,0,1:T(8,128)(2,1)S(1)}, u32[]{:S(2)}, u32[]{:S(2)}) async-start(bf16[8,16,3584]{2,0,1:T(8,128)(2,1)} %bitcast.53), calls=%async_computation | async-start | bytes 1835008 | tf_op jit(solution)/shard_map/all_to_all | solution.py:49
  113.2 81.9 %reduce-scatter.5.cloned.1.call-done = bf16[1792,768]{0,1:T(8,128)(2,1)} async-done(((bf16[3584,768]{0,1:T(8,128)(2,1)}), bf16[1792,768]{0,1:T(8,128)(2,1)}) %reduce-scatter.5.cloned.1.call-update) | async-done | bytes 2752528 | tf_op jit(solution)/shard_map/reduce_scatter | solution.py:57
  195.1 3.3 %slice_bitcast_fusion = (bf16[1,1792,256]{1,2,0:T(8,128)(2,1)}, bf16[1,1792,256]{1,2,0:T(8,128)(2,1)}, bf16[1,1792,256]{1,2,0:T(8,128)(2,1)}) fusion(bf16[1792,768]{0,1:T(8,128)(2,1)} %reduce-scatter.5.cloned.1.call-done), kind=kLoop, calls=%fused_computation.25 | loop fusion | bytes 5505024 | tf_op jit(solution)/shard_map/broadcast_in_dim | solution.py:65
  198.4 2.2 %copy.31 = bf16[1,1792,256]{2,1,0:T(8,128)(2,1)} copy(bf16[1,1792,256]{1,2,0:T(8,128)(2,1)} %get-tuple-element.22) | data formatting | bytes 1835008
  200.6 2.2 %copy.32 = bf16[1,1792,256]{2,1,0:T(8,128)(2,1)} copy(bf16[1,1792,256]{1,2,0:T(8,128)(2,1)} %get-tuple-element.21) | data formatting | bytes 1835008
  202.8 2.2 %copy.33 = bf16[1,1792,256]{2,1,0:T(8,128)(2,1)} copy(bf16[1,1792,256]{1,2,0:T(8,128)(2,1)} %get-tuple-element.20) | data formatting | bytes 1835008
  205.1 0.0 all-to-all-done
  205.1 1.2 copy.30
  206.3 0.0 copy-done.1
  (3 shorter events, 0.0 us)
Async XLA Ops:
  7.2 1.5 copy-start
  7.2 96.6 %reduce-scatter.7.cloned.1.call-start = ((), (), s32[]{:S(2)}) async-start(), calls=%async_computation.4 | async-start | bytes 8257536
  8.7 6.3 %copy-start.2 = (bf16[1,3584,256]{2,1,0:T(8,128)(2,1)S(1)}, bf16[1,3584,256]{2,1,0:T(8,128)(2,1)}, u32[]{:S(2)}) copy-start(bf16[1,3584,256]{2,1,0:T(8,128)(2,1)} %param.12) | copy-start | bytes 5505028
  8.7 6.3 %copy-start.6 = (bf16[1,1,64,16,3584]{4,3,2,1,0:T(8,128)(2,1)S(1)}, bf16[1,1,64,16,3584]{4,3,2,1,0:T(8,128)(2,1)}, u32[]{:S(2)}) copy-start(bf16[1,1,64,16,3584]{4,3,2,1,0:T(8,128)(2,1)} %param.7) | copy-start | bytes 22020100
  15.0 3.1 %copy-start.4 = (f32[1,1,64,16]{2,3,1,0:T(8,128)S(1)}, f32[1,1,64,16]{2,3,1,0:T(8,128)}, u32[]{:S(2)}) copy-start(f32[1,1,64,16]{2,3,1,0:T(8,128)} %param.9) | copy-start | bytes 12292
  15.0 3.1 %copy-start.5 = (s32[1,1,16]{2,1,0:T(1,128)S(1)}, s32[1,1,16]{2,1,0:T(1,128)}, u32[]{:S(2)}) copy-start(s32[1,1,16]{2,1,0:T(1,128)} %param.10) | copy-start | bytes 196
  28.3 7.3 %copy-start.3 = (bf16[1,3584,256]{2,1,0:T(8,128)(2,1)S(1)}, bf16[1,3584,256]{2,1,0:T(8,128)(2,1)}, u32[]{:S(2)}) copy-start(bf16[1,3584,256]{2,1,0:T(8,128)(2,1)} %param.12) | copy-start | bytes 5505028
  50.4 144.7 %reduce-scatter.5.cloned.1.call-start = ((), (), s32[]{:S(2)}) async-start(), calls=%async_computation.3 | async-start | bytes 8257536 | tf_op jit(solution)/shard_map/reduce_scatter | solution.py:57
  103.8 102.5 %copy-start.1 = (bf16[1,3584,256]{2,1,0:T(8,128)(2,1)S(1)}, bf16[1,3584,256]{2,1,0:T(8,128)(2,1)}, u32[]{:S(2)}) copy-start(bf16[1,3584,256]{2,1,0:T(8,128)(2,1)} %param.11) | copy-start | bytes 5505028
  103.8 101.3 %all-to-all-start = ((bf16[8,16,3584]{2,0,1:T(8,128)(2,1)}), bf16[8,16,3584]{2,0,1:T(8,128)(2,1)S(1)}, u32[]{:S(2)}, u32[]{:S(2)}) async-start(bf16[8,16,3584]{2,0,1:T(8,128)(2,1)} %bitcast.53), calls=%async_computation | async-start | bytes 1835008 | tf_op jit(solution)/shard_map/all_to_all | solution.py:49
Sparse Core Ops, SparseCore 0:
  50.5 53.2 reduce-scatter.6
  106.3 88.7 reduce-scatter.4
where the time goes:
time: 214 us; the launch traced here: 213 us
  waiting for transfers between devices  115 us (54%)
  matrix products  40.2 us (19%)
  local copies, waits for them, and re-layouts  20.2 us (9%)
  between operations  14.1 us (7%)
  other arithmetic  13.9 us (6%)
  starting transfers between devices  9.47 us (4%)
    reduce_scatter x1, waiting for transfers between devices, on_device(): lax.psum_scatter(jnp.concatenate((front, behind), axis=1).astype(jnp.bflo...  81.9 us
    unnamed x3, waiting for transfers between devices  33.2 us
    unnamed x20, local copies, waits for them, and re-layouts  16.5 us
    convert_element_type x2, other arithmetic, on_device(): scaled_rows = (grad_rows[0, 0].astype(jnp.float32) * (combine_weights[0,...  11.1 us
    all_to_all x1, starting transfers between devices, on_device(): lax.all_to_all(summed, 'node', split_axis=1, concat_axis=1, tiled=True)  9.39 us
    dot_general x1, matrix products, on_device(): lax.dot_general(flat_tokens, joined_grad, (((0,), (0,)), ((), ())), prefe...  7.78 us
    dot_general x1, matrix products, on_device(): lax.dot_general(up_grad, up_weight, (((1,), (1,)), ((), ())), preferred_e...  7.51 us
    dot_general x1, matrix products, on_device(): lax.dot_general(gate_grad, gate_weight, (((1,), (1,)), ((), ())), preferr...  7.33 us
  transfers between devices with their start and end apart: 3, of which 2 were waited for; matrix products, arithmetic and copies ran while one was open for 14% of the time, Pallas kernels for 0%

commit v1 on v0

--- a/solution.py
+++ b/solution.py
@@ -46,7 +46,10 @@
         scatter_dimension=0,
         tiled=True,
     )
-    returned = lax.all_to_all(summed, "node", split_axis=1, concat_axis=1, tiled=True)
+    returned = jnp.concatenate(
+        lax.all_to_all(jnp.stack(jnp.split(summed, lax.axis_size("node"), axis=1)), "node", 0, 0),
+        axis=1,
+    )
     d_tokens = returned[None, None]
     front = lax.dot_general(
         flat_tokens, joined_grad, (((0,), (0,)), ((), ())), preferred_element_type=jnp.float32

time: 214 us -> 219 us (1.023)
  local copies, waits for them, and re-layouts: 20.2 us -> 43.4 us
  waiting for transfers between devices: 115 us -> 96.8 us
    unnamed x20 -> x35, local copies, waits for them, and re-layouts: 16.5 us -> 38.2 us
    reduce_scatter x1, waiting for transfers between devices: 81.9 us -> 63.6 us  [on_device(): lax.psum_scatter(jnp.concatenate((front, behind), axis=1).astype(jnp.bflo...]
  transfers between devices with their start and end apart: 3 -> 3, of which waited for: 2 -> 2; matrix products, arithmetic and copies ran while one was open for 14% -> 24% of each run, Pallas kernels for 0% -> 0%
where the time goes in v1:
time: 219 us; the launch traced here: 218 us
  waiting for transfers between devices  96.8 us (44%)
  local copies, waits for them, and re-layouts  43.4 us (20%)
  matrix products  40.2 us (18%)
  between operations  14.1 us (6%)
  other arithmetic  13.9 us (6%)
  starting transfers between devices  9.34 us (4%)
    reduce_scatter x1, waiting for transfers between devices, on_device(): lax.psum_scatter(jnp.concatenate((front, behind), axis=1).astype(jnp.bflo...  63.6 us
    unnamed x35, local copies, waits for them, and re-layouts  38.2 us
    unnamed x3, waiting for transfers between devices  33.3 us
    convert_element_type x2, other arithmetic, on_device(): scaled_rows = (grad_rows[0, 0].astype(jnp.float32) * (combine_weights[0,...  11.1 us
    all_to_all x1, starting transfers between devices, on_device(): lax.all_to_all(jnp.stack(jnp.split(summed, lax.axis_size('node'), axis=1)...  9.26 us
    dot_general x1, matrix products, on_device(): lax.dot_general(flat_tokens, joined_grad, (((0,), (0,)), ((), ())), prefe...  7.74 us
    dot_general x1, matrix products, on_device(): lax.dot_general(up_grad, up_weight, (((1,), (1,)), ((), ())), preferred_e...  7.51 us
    dot_general x1, matrix products, on_device(): lax.dot_general(gate_grad, gate_weight, (((1,), (1,)), ((), ())), preferr...  7.33 us
  transfers between devices with their start and end apart: 3, of which 2 were waited for; matrix products, arithmetic and copies ran while one was open for 24% of the time, Pallas kernels for 0%

profile of v1, /device:TPU:1, one launch (start us, length us, event | category | flops | bytes accessed | tf_op | source)
XLA Modules:
  0.0 217.9 jit_solution(16130116428871042441)
XLA Ops:
  7.2 0.0 copy-start
  7.2 0.0 reduce-scatter.7.cloned.1.call-start
  7.2 1.4 copy-done
  8.7 6.3 %fusion.4 = f32[1024,256]{0,1:T(8,128)} fusion(bf16[1024,3584]{1,0:T(8,128)(2,1)} %bitcast.137, bf16[1,3584,256]{2,1,0:T(8,128)(2,1)S(1)} %copy-done), kind=kOutput, calls=%fused_computation.10 | convolution fusion | flops 1879048192 | bytes 10223616 | tf_op jit(solution)/shard_map/dot_general | solution.py:23
  15.0 3.1 %fusion.7 = f32[1024,256]{0,1:T(8,128)} fusion(bf16[1024,3584]{1,0:T(8,128)(2,1)S(1)} %bitcast.139, bf16[1,3584,256]{2,1,0:T(8,128)(2,1)S(1)} %copy-done.2), kind=kOutput, calls=%fused_computation.13 | convolution fusion | flops 1879048192 | bytes 10223616 | tf_op jit(solution)/shard_map/dot_general | solution.py:24
  18.1 0.1 bitcast_select_fusion
  18.2 0.1 copy.38
  18.2 5.6 %multiply_convert_fusion = bf16[1,1,64,16,3584]{4,3,2,1,0:T(8,128)(2,1)S(1)} fusion(f32[64,16]{1,0:T(8,128)S(1)} %copy.38, bf16[1,1,64,16,3584]{4,3,2,1,0:T(8,128)(2,1)} %param.8), kind=kLoop, calls=%fused_computation.3 | loop fusion | flops 11010048 | bytes 14684160 | tf_op jit(solution)/shard_map/convert_element_type | solution.py:20
  23.8 4.5 %multiply_convert_fusion.2 = (bf16[1024,256]{0,1:T(8,128)(2,1)S(1)}, bf16[1024,256]{0,1:T(8,128)(2,1)S(1)}) fusion(f32[1024,256]{0,1:T(8,128)} %fusion.4, f32[1024,256]{0,1:T(8,128)} %fusion.7, bf16[1024,3584]{1,0:T(8,128)(2,1)S(1)} %bitcast.117, bf16[1,3584,256]{2,1,0:T(8,128)(2,1)} %param.13), kind=kOutput, calls=%fused_computation.21 | convolution fusion | flops 1882456064 | bytes 12320768 | tf_op jit(solution)/shard_map/dot_general | solution.py:28
  28.3 0.0 copy-start.3
  28.4 7.3 %fusion.2 = f32[1024,3584]{1,0:T(8,128)} fusion(bf16[1024,256]{0,1:T(8,128)(2,1)S(1)} %get-tuple-element.20, bf16[1,3584,256]{2,1,0:T(8,128)(2,1)S(1)} %copy-done), kind=kOutput, calls=%fused_computation.8 | convolution fusion | flops 1879048192 | bytes 17039360 | tf_op jit(solution)/shard_map/dot_general | solution.py:35
  35.7 7.5 %add_convert_fusion = bf16[1024,3584]{1,0:T(8,128)(2,1)S(1)} fusion(f32[1024,3584]{1,0:T(8,128)} %fusion.2, bf16[1024,256]{0,1:T(8,128)(2,1)S(1)} %get-tuple-element.19, bf16[1,3584,256]{2,1,0:T(8,128)(2,1)S(1)} %copy-done.3), kind=kOutput, calls=%fused_computation.2 | convolution fusion | flops 1886388224 | bytes 24379392 | tf_op jit(solution)/shard_map/dot_general | solution.py:38
  43.2 7.1 %copy.47 = bf16[8,8,16,3584]{3,1,2,0:T(8,128)(2,1)} copy(bf16[8,8,16,3584]{3,2,1,0:T(8,128)(2,1)S(1)} %bitcast.116) | data formatting | bytes 14680064
  50.4 0.0 reduce-scatter.7.cloned.1.call-update
  50.4 0.0 reduce-scatter.5.cloned.1.call-start
  50.4 0.1 copy.40
  50.5 0.1 lt.25
  50.6 0.1 iota.15
  50.7 0.1 squeeze.19
  50.8 5.5 %fusion = bf16[1024,3584]{1,0:T(8,128)(2,1)S(1)} fusion(f32[1024]{0:T(1024)S(1)} %compare_select_fusion, bf16[1,1,64,16,3584]{4,3,2,1,0:T(8,128)(2,1)} %param.8), kind=kLoop, calls=%fused_computation.1 | loop fusion | flops 11010048 | bytes 14684160 | tf_op jit(solution)/shard_map/convert_element_type | solution.py:20
  56.3 3.7 %convolution_convert_fusion.1 = bf16[3584,256]{0,1:T(8,128)(2,1)S(1)} fusion(bf16[1024,3584]{1,0:T(8,128)(2,1)S(1)} %fusion, f32[1024,256]{0,1:T(8,128)} %fusion.7, f32[1024,256]{0,1:T(8,128)} %fusion.4), kind=kOutput, calls=%fused_computation.7 | convolution fusion | flops 1881538560 | bytes 11272192 | tf_op jit(solution)/shard_map/dot_general | solution.py:57
  60.0 7.7 %fusion.1 = bf16[3584,512]{0,1:T(8,128)(2,1)S(1)} fusion(bf16[1024,3584]{1,0:T(8,128)(2,1)} %bitcast.138, bf16[1024,256]{0,1:T(8,128)(2,1)S(1)} %get-tuple-element.19, bf16[1024,256]{0,1:T(8,128)(2,1)S(1)} %get-tuple-element.20), kind=kOutput, calls=%fused_computation.6 | convolution fusion | flops 3762028544 | bytes 12058624 | tf_op jit(solution)/shard_map/dot_general | solution.py:54
  67.8 2.7 %pad_maximum_fusion = bf16[3584,768]{0,1:T(8,128)(2,1)} fusion(bf16[3584,256]{0,1:T(8,128)(2,1)S(1)} %convolution_convert_fusion.1, bf16[3584,512]{0,1:T(8,128)(2,1)S(1)} %fusion.1), kind=kLoop, calls=%fused_computation.5 | loop fusion | flops 11010048 | bytes 11010048 | tf_op jit(solution)/shard_map/concatenate | solution.py:61
  70.5 0.0 reduce-scatter.5.cloned.1.call-update
  70.5 33.2 %reduce-scatter.7.cloned.1.call-done = bf16[8,57344]{1,0:T(8,128)(2,1)} async-done(((bf16[64,57344]{1,0:T(8,128)(2,1)}), bf16[8,57344]{1,0:T(8,128)(2,1)}) %reduce-scatter.7.cloned.1.call-update) | async-done | bytes 917520
  103.8 1.4 fusion.31
  105.2 1.4 fusion.30
  106.7 1.4 fusion.29
  108.1 1.4 fusion.28
  109.6 1.4 fusion.27
  111.0 1.4 fusion.26
  112.4 1.4 fusion.25
  113.9 1.4 fusion.24
  115.3 1.4 fusion.23
  116.8 1.4 fusion.22
  118.2 1.5 fusion.21
  119.7 1.4 fusion.20
  121.1 1.4 fusion.19
  122.6 1.4 fusion.18
  124.0 1.4 fusion.17
  125.5 1.6 fusion.16
  127.0 9.3 %all-to-all-start = ((bf16[16,8,1,3584]{3,1,2,0:T(8,128)(2,1)}), bf16[16,8,1,3584]{3,1,2,0:T(8,128)(2,1)S(1)}, u32[]{:S(2)}, u32[]{:S(2)}) async-start(bf16[16,8,1,3584]{3,1,2,0:T(8,128)(2,1)} %fusion.16), calls=%async_computation | async-start | bytes 1835008 | tf_op jit(solution)/shard_map/all_to_all | solution.py:50
  136.3 63.6 %reduce-scatter.5.cloned.1.call-done = bf16[1792,768]{0,1:T(8,128)(2,1)} async-done(((bf16[3584,768]{0,1:T(8,128)(2,1)}), bf16[1792,768]{0,1:T(8,128)(2,1)}) %reduce-scatter.5.cloned.1.call-update) | async-done | bytes 2752528 | tf_op jit(solution)/shard_map/reduce_scatter | solution.py:60
  199.9 3.3 %slice_bitcast_fusion = (bf16[1,1792,256]{1,2,0:T(8,128)(2,1)}, bf16[1,1792,256]{1,2,0:T(8,128)(2,1)}, bf16[1,1792,256]{1,2,0:T(8,128)(2,1)}) fusion(bf16[1792,768]{0,1:T(8,128)(2,1)} %reduce-scatter.5.cloned.1.call-done), kind=kLoop, calls=%fused_computation.25 | loop fusion | bytes 5505024 | tf_op jit(solution)/shard_map/broadcast_in_dim | solution.py:68
  203.2 2.2 %copy.42 = bf16[1,1792,256]{2,1,0:T(8,128)(2,1)} copy(bf16[1,1792,256]{1,2,0:T(8,128)(2,1)} %get-tuple-element.18) | data formatting | bytes 1835008
  205.4 2.2 %copy.43 = bf16[1,1792,256]{2,1,0:T(8,128)(2,1)} copy(bf16[1,1792,256]{1,2,0:T(8,128)(2,1)} %get-tuple-element.17) | data formatting | bytes 1835008
  207.6 2.2 %copy.44 = bf16[1,1792,256]{2,1,0:T(8,128)(2,1)} copy(bf16[1,1792,256]{1,2,0:T(8,128)(2,1)} %get-tuple-element.16) | data formatting | bytes 1835008
  209.8 1.2 copy.41
  (15 shorter events, 0.0 us)
Async XLA Ops:
  7.2 1.5 copy-start
  7.2 96.6 %reduce-scatter.7.cloned.1.call-start = ((), (), s32[]{:S(2)}) async-start(), calls=%async_computation.4 | async-start | bytes 8257536
  8.7 6.3 %copy-start.2 = (bf16[1,3584,256]{2,1,0:T(8,128)(2,1)S(1)}, bf16[1,3584,256]{2,1,0:T(8,128)(2,1)}, u32[]{:S(2)}) copy-start(bf16[1,3584,256]{2,1,0:T(8,128)(2,1)} %param.12) | copy-start | bytes 5505028
  8.7 6.3 %copy-start.6 = (bf16[1,1,64,16,3584]{4,3,2,1,0:T(8,128)(2,1)S(1)}, bf16[1,1,64,16,3584]{4,3,2,1,0:T(8,128)(2,1)}, u32[]{:S(2)}) copy-start(bf16[1,1,64,16,3584]{4,3,2,1,0:T(8,128)(2,1)} %param.7) | copy-start | bytes 22020100
  15.0 3.1 %copy-start.4 = (f32[1,1,64,16]{2,3,1,0:T(8,128)S(1)}, f32[1,1,64,16]{2,3,1,0:T(8,128)}, u32[]{:S(2)}) copy-start(f32[1,1,64,16]{2,3,1,0:T(8,128)} %param.9) | copy-start | bytes 12292
  15.0 3.1 %copy-start.5 = (s32[1,1,16]{2,1,0:T(1,128)S(1)}, s32[1,1,16]{2,1,0:T(1,128)}, u32[]{:S(2)}) copy-start(s32[1,1,16]{2,1,0:T(1,128)} %param.10) | copy-start | bytes 196
  28.3 7.3 %copy-start.3 = (bf16[1,3584,256]{2,1,0:T(8,128)(2,1)S(1)}, bf16[1,3584,256]{2,1,0:T(8,128)(2,1)}, u32[]{:S(2)}) copy-start(bf16[1,3584,256]{2,1,0:T(8,128)(2,1)} %param.12) | copy-start | bytes 5505028
  50.4 149.5 %reduce-scatter.5.cloned.1.call-start = ((), (), s32[]{:S(2)}) async-start(), calls=%async_computation.3 | async-start | bytes 8257536 | tf_op jit(solution)/shard_map/reduce_scatter | solution.py:60
  125.5 85.6 %copy-start.1 = (bf16[1,3584,256]{2,1,0:T(8,128)(2,1)S(1)}, bf16[1,3584,256]{2,1,0:T(8,128)(2,1)}, u32[]{:S(2)}) copy-start(bf16[1,3584,256]{2,1,0:T(8,128)(2,1)} %param.11) | copy-start | bytes 5505028
  127.0 82.8 %all-to-all-start = ((bf16[16,8,1,3584]{3,1,2,0:T(8,128)(2,1)}), bf16[16,8,1,3584]{3,1,2,0:T(8,128)(2,1)S(1)}, u32[]{:S(2)}, u32[]{:S(2)}) async-start(bf16[16,8,1,3584]{3,1,2,0:T(8,128)(2,1)} %fusion.16), calls=%async_computation | async-start | bytes 1835008 | tf_op jit(solution)/shard_map/all_to_all | solution.py:50
Sparse Core Ops, SparseCore 0:
  50.5 53.2 reduce-scatter.6
  106.3 93.4 reduce-scatter.4
